TPU v7x, 32 devices: a whole 2x2x4 slice. The times are simulated.
32 devices in a mesh: view: 4 (over y, x), blk: 8 (over z, core).
Axes of the slice: x: 2, y: 2, z: 4, core: 2. Of those that a mesh axis runs over, the one named last changes fastest.
Arguments:
- estimate: float32 [384, 64, 256], P('blk'), may hold values from 0.5 to 2
- views_seen: float32 [4, 384, 64, 256], P('view', 'blk'), may hold values from 0.2 to 5
- weight_mask: int32 [4, 384, 64, 256], P('view', 'blk'), may hold values from 1 to 3
- psf: float32 [4, 3, 21], P('view'), may hold values from 0.05 to 1
Outputs:
- joined: float32 [384, 64, 256], P('blk')
All inputs are finite; a program needn't handle non-finite values.
Results may differ from a plain program's by a relative error of at most 0.0001.
Values sent between devices are 32-bit elements; how exact they have to be, the bound alone decides.
A program may use at most 128 MiB of HBM per device.

v0:
```python
import jax
import jax.numpy as jnp
from jax import lax
from jax.sharding import PartitionSpec as P

ITERS = 2


def extended(cells, sides, width):
    for axis, dim in sides:
        count = lax.axis_size(axis)
        ends = count - 1
        head = lax.slice_in_dim(cells, 0, width, axis=dim)
        tail = lax.slice_in_dim(cells, cells.shape[dim] - width, cells.shape[dim], axis=dim)
        cells = jnp.concatenate(
            [
                lax.ppermute(tail, axis, [(i, (i + 1) % count) for i in range(ends)]),
                cells,
                lax.ppermute(head, axis, [((i + 1) % count, i) for i in range(ends)]),
            ],
            axis=dim,
        )
    return cells


def band_matrix(kernel, out_count, in_count, offset_by):
    row_index = jnp.arange(out_count)[:, None]
    col_index = jnp.arange(in_count)[None, :]
    offset_table = col_index - row_index + offset_by
    matches = offset_table[:, :, None] == jnp.arange(kernel.shape[0])[None, None, :]
    return jnp.sum(jnp.where(matches, kernel[None, None, :], 0.0), axis=-1)


def sweep_first(padded, kernel, count):
    result = kernel[0] * padded[0:count]
    for tap in range(1, kernel.shape[0]):
        result = result + kernel[tap] * padded[tap : tap + count]
    return result


def sweep_rest(volume, kernel):
    radius = (kernel.shape[-1] - 1) // 2
    along_y = band_matrix(kernel[1], volume.shape[1], volume.shape[1], radius)
    volume = jnp.einsum("ij,xjz->xiz", along_y, volume, precision=lax.Precision.HIGHEST)
    along_z = band_matrix(kernel[2], volume.shape[2], volume.shape[2], radius)
    return jnp.einsum("xyj,kj->xyk", volume, along_z, precision=lax.Precision.HIGHEST)


def body(estimate, views_seen, weight_mask, psf):
    slab = estimate.shape[0]
    radius = (psf.shape[-1] - 1) // 2
    normed = psf / jnp.sum(psf, axis=-1, keepdims=True)
    flipped = normed[:, :, ::-1]
    weights_all = lax.psum(jnp.sum(weight_mask.astype(jnp.float32), axis=0), "view")
    for iteration in range(ITERS):
        padded = extended(estimate, (("blk", 0),), radius)
        forward = normed[0]
        backward = flipped[0]
        blurred = sweep_rest(sweep_first(padded, forward[0], slab), forward)
        quotient = views_seen[0] / blurred
        quotient_wide = extended(quotient, (("blk", 0),), radius)
        correction = sweep_rest(sweep_first(quotient_wide, backward[0], slab), backward)
        numerator = weight_mask[0].astype(jnp.float32) * correction
        summed = lax.psum(numerator, "view")
        estimate = estimate * summed / weights_all
    return estimate


def solution(mesh):
    placed = (
        P("blk", None, None),
        P("view", "blk", None, None),
        P("view", "blk", None, None),
        P("view", None, None),
    )
    return jax.shard_map(
        body, mesh=mesh, in_specs=placed, out_specs=P("blk", None, None), check_vma=False
    )
```

profile of v0, /device:TPU:20, one launch (start us, length us, event | category | flops | bytes accessed | tf_op | source)
XLA Modules:
  0.0 505.9 jit_solution(5480964015441795965)
XLA Ops:
  6.5 0.0 all-reduce.6.cloned.1.call-start
  6.5 2.6 fusion.403
  9.1 1.9 collective-permute-start
  11.1 3.6 collective-permute-start.1
  14.7 0.8 reduce_sum.43
  15.5 0.8 broadcast_divide_fusion
  16.3 0.7 fusion.404
  17.0 0.6 fusion.405
  17.6 0.1 slice.671
  17.7 0.1 slice.672
  17.8 0.2 select_reduce_fusion.2
  18.1 1.0 select_reduce_fusion
  19.0 0.0 copy-start.6
  19.0 2.3 collective-permute-done
  21.4 1.1 constant_dynamic-update-slice_fusion.1
  22.5 0.0 copy-done.1
  22.5 0.5 constant_dynamic-update-slice_fusion
  23.0 0.0 copy-start.7
  23.0 0.1 collective-permute-done.1
  23.1 1.6 constant_dynamic-update-slice_fusion.2
  24.7 0.1 copy-done.7
  24.8 30.9 %fusion.244 = f32[48,256,64]{1,2,0:T(8,128)} fusion(f32[58,64,256]{2,1,0:T(8,128)S(1)} %constant_dynamic-update-slice_fusion.2, f32[58,64,256]{2,1,0:T(8,128)} %copy-done.7, f32[48,64,256]{2,1,0:T(8,128)S(1)} %copy-done.1, f32[]{:T(128)} %bitcast.22, f32[]{:T(128)} %bitcast.21, f32[]{:T(128)} %bitcast.20, f32[]{:T(128)} %bitcast.19, f32[]{:T(128)} %bitcast.18, ...), kind=kOutput, calls=%fused_computation.302 | convolution fusion | flops 636223488 | bytes 69249536 | tf_op jit(solution)/shard_map/ij,xjz->xiz/dot_general | solution.py:44
  55.7 0.0 copy-done.6
  55.7 0.0 copy-start
  55.7 5.9 %bitcast_divide_fusion.1 = f32[48,64,256]{2,1,0:T(8,128)S(1)} fusion(f32[1,48,64,256]{3,2,1,0:T(8,128)} %param.5, f32[48,256,64]{1,2,0:T(8,128)} %fusion.244, f32[256,256]{1,0:T(8,128)S(1)} %get-tuple-element.6), kind=kOutput, calls=%fused_computation.350 | convolution fusion | flops 2416705536 | bytes 9699328 | tf_op jit(solution)/shard_map/xyj,kj->xyk/dot_general | solution.py:46
  61.6 0.0 copy-start.5
  61.6 0.1 fusion.402
  61.7 3.2 collective-permute-start.2
  64.9 2.6 collective-permute-start.3
  67.4 0.0 copy-done
  67.5 2.0 convert_bitcast_fusion
  69.5 0.0 copy-done.5
  69.5 4.1 collective-permute-done.2
  73.6 1.8 collective-permute-done.3
  75.3 0.0 copy-done.9
  75.4 0.8 copy-done.11
  76.2 44.5 %fusion.154 = f32[48,256,64]{1,2,0:T(8,128)} fusion(f32[48,64,256]{2,1,0:T(8,128)} %copy-done.5, f32[10,64,256]{2,1,0:T(8,128)} %copy-done.11, f32[10,64,256]{2,1,0:T(8,128)} %copy-done.9, f32[]{:T(128)} %bitcast.22, f32[]{:T(128)} %bitcast.21, f32[]{:T(128)} %bitcast.20, f32[]{:T(128)} %bitcast.19, f32[]{:T(128)} %bitcast.18, f32[]{:T(128)} %bitcast.17, ...), kind=kOutput, calls=%fused_computation.229 | convolution fusion | flops 651952128 | bytes 7618644 | tf_op jit(solution)/shard_map/ij,xjz->xiz/dot_general | solution.py:44
  120.7 6.2 %fusion.295 = f32[48,64,256]{2,1,0:T(8,128)} fusion(f32[48,256,64]{1,2,0:T(8,128)} %fusion.154, f32[256,256]{1,0:T(8,128)S(1)} %get-tuple-element.5, s32[1,48,64,256]{3,2,1,0:T(8,128)S(1)} %copy-done), kind=kOutput, calls=%fused_computation.358 | convolution fusion | flops 2417491968 | bytes 9699328 | tf_op jit(solution)/shard_map/xyj,kj->xyk/dot_general | solution.py:46
  127.0 0.0 all-reduce.6.cloned.1.call-update
  127.0 0.0 all-reduce.4.cloned.1.call-start
  127.0 140.2 %all-reduce.6.cloned.1.call-done = (f32[48,64,256]{2,1,0:T(8,128)}, f32[48,64,256]{2,1,0:T(8,128)}) async-done(((f32[48,64,256]{2,1,0:T(8,128)}, f32[48,64,256]{2,1,0:T(8,128)}), (f32[48,64,256]{2,1,0:T(8,128)}, f32[48,64,256]{2,1,0:T(8,128)})) %all-reduce.6.cloned.1.call-update) | async-done | bytes 6291472 | tf_op jit(solution)/shard_map/psum | solution.py:54
  267.2 4.7 multiply_divide_fusion.1
  271.9 0.0 copy-start.2
  271.9 1.7 copy-done.2
  273.5 0.1 fusion.401
  273.7 1.9 collective-permute-start.4
  275.6 3.9 collective-permute-start.5
  279.5 6.1 %collective-permute-done.4 = f32[10,64,256]{2,1,0:T(8,128)S(1)} collective-permute-done((f32[10,64,256]{2,1,0:T(8,128)S(1)}, f32[10,64,256]{2,1,0:T(8,128)S(1)}, u32[]{:S(2)}, u32[]{:S(2)}) %collective-permute-start.4) | collective-permute-done | bytes 655392 | tf_op jit(solution)/shard_map/ppermute | solution.py:17
  285.6 0.8 copy-done.10
  286.4 0.9 collective-permute-done.5
  287.3 45.2 %fusion.79 = f32[48,256,64]{1,2,0:T(8,128)} fusion(f32[48,64,256]{2,1,0:T(8,128)} %copy-done.2, f32[10,64,256]{2,1,0:T(8,128)} %collective-permute-done.5, f32[10,64,256]{2,1,0:T(8,128)} %copy-done.10, f32[]{:T(128)} %bitcast.22, f32[]{:T(128)} %bitcast.21, f32[]{:T(128)} %bitcast.20, f32[]{:T(128)} %bitcast.19, f32[]{:T(128)} %bitcast.18, f32[]{:T(128)} %bitcast.17, ...), kind=kOutput, calls=%fused_computation.172 | convolution fusion | flops 651952128 | bytes 7618644 | tf_op jit(solution)/shard_map/ij,xjz->xiz/dot_general | solution.py:44
  332.5 5.8 %bitcast_divide_fusion = f32[48,64,256]{2,1,0:T(8,128)S(1)} fusion(f32[1,48,64,256]{3,2,1,0:T(8,128)} %param.5, f32[48,256,64]{1,2,0:T(8,128)} %fusion.79, f32[256,256]{1,0:T(8,128)} %copy-done.6), kind=kOutput, calls=%fused_computation.349 | convolution fusion | flops 2416705536 | bytes 9699328 | tf_op jit(solution)/shard_map/xyj,kj->xyk/dot_general | solution.py:46
  338.3 0.0 copy-start.4
  338.3 0.1 fusion.400
  338.4 3.8 collective-permute-start.6
  342.2 2.3 collective-permute-start.7
  344.6 6.1 %collective-permute-done.6 = f32[10,64,256]{2,1,0:T(8,128)S(1)} collective-permute-done((f32[10,64,256]{2,1,0:T(8,128)S(1)}, f32[10,64,256]{2,1,0:T(8,128)S(1)}, u32[]{:S(2)}, u32[]{:S(2)}) %collective-permute-start.6) | collective-permute-done | bytes 655392 | tf_op jit(solution)/shard_map/ppermute | solution.py:17
  350.6 0.9 copy-done.8
  351.5 0.9 collective-permute-done.7
  352.4 46.7 %fusion.4 = f32[48,256,64]{1,2,0:T(8,128)} fusion(f32[48,64,256]{2,1,0:T(8,128)} %copy-done.4, f32[10,64,256]{2,1,0:T(8,128)} %collective-permute-done.7, f32[10,64,256]{2,1,0:T(8,128)} %copy-done.8, f32[]{:T(128)} %bitcast.22, f32[]{:T(128)} %bitcast.21, f32[]{:T(128)} %bitcast.20, f32[]{:T(128)} %bitcast.19, f32[]{:T(128)} %bitcast.18, f32[]{:T(128)} %bitcast.17, ...), kind=kOutput, calls=%fused_computation.115 | convolution fusion | flops 651952128 | bytes 7618644 | tf_op jit(solution)/shard_map/ij,xjz->xiz/dot_general | solution.py:44
  399.0 6.2 %fusion.298 = f32[48,64,256]{2,1,0:T(8,128)} fusion(f32[48,256,64]{1,2,0:T(8,128)} %fusion.4, f32[256,256]{1,0:T(8,128)S(1)} %get-tuple-element.5, s32[1,48,64,256]{3,2,1,0:T(8,128)S(1)} %copy-done), kind=kOutput, calls=%fused_computation.359 | convolution fusion | flops 2417491968 | bytes 9699328 | tf_op jit(solution)/shard_map/xyj,kj->xyk/dot_general | solution.py:46
  405.3 0.0 all-reduce.4.cloned.1.call-update
  405.3 88.0 %all-reduce.4.cloned.1.call-done = f32[48,64,256]{2,1,0:T(8,128)} async-done(((f32[48,64,256]{2,1,0:T(8,128)}), f32[48,64,256]{2,1,0:T(8,128)}) %all-reduce.4.cloned.1.call-update) | async-done | bytes 3145744 | tf_op jit(solution)/shard_map/psum | solution.py:64
  493.3 5.7 %multiply_divide_fusion = f32[48,64,256]{2,1,0:T(8,128)} fusion(f32[48,64,256]{2,1,0:T(8,128)} %get-tuple-element.9, f32[48,64,256]{2,1,0:T(8,128)S(1)} %copy-done.3, f32[48,64,256]{2,1,0:T(8,128)} %all-reduce.4.cloned.1.call-done), kind=kLoop, calls=%fused_computation.351 | loop fusion | flops 1572864 | bytes 12582912 | tf_op jit(solution)/shard_map/div | solution.py:65
  (11 shorter events, 0.1 us)
Async XLA Ops:
  6.5 16.0 %copy-start.1 = (f32[48,64,256]{2,1,0:T(8,128)S(1)}, f32[48,64,256]{2,1,0:T(8,128)}, u32[]{:S(2)}) copy-start(f32[48,64,256]{2,1,0:T(8,128)} %param.4) | copy-start | bytes 9437188
  6.5 260.7 %all-reduce.6.cloned.1.call-start = ((), (), s32[]{:S(2)}) async-start(), calls=%async_computation.1 | async-start | bytes 12582912 | tf_op jit(solution)/shard_map/psum | solution.py:54
  9.1 12.2 %collective-permute-start = (f32[10,64,256]{2,1,0:T(8,128)}, f32[10,64,256]{2,1,0:T(8,128)}, u32[]{:S(2)}, u32[]{:S(2)}) collective-permute-start(f32[10,64,256]{2,1,0:T(8,128)} %get-tuple-element.19), channel_id=1, source_target_pairs={{0,1},{1,2},{2,3},{3,4},{4,5},{5,6},{6,7},{8,9},{9,10},{10,11},{11... | collective-permute-start | bytes 1966088 | tf_op jit(solution)/shard_map/ppermute | solution.py:17
  11.1 12.0 %collective-permute-start.1 = (f32[10,64,256]{2,1,0:T(8,128)}, f32[10,64,256]{2,1,0:T(8,128)}, u32[]{:S(2)}, u32[]{:S(2)}) collective-permute-start(f32[10,64,256]{2,1,0:T(8,128)} %get-tuple-element.20), channel_id=1, source_target_pairs={{1,0},{2,1},{3,2},{4,3},{5,4},{6,5},{7,6},{9,8},{10,9},{11,10},{12... | collective-permute-start | bytes 1966088 | tf_op jit(solution)/shard_map/ppermute | solution.py:19
  19.0 36.7 %copy-start.6 = (f32[256,256]{1,0:T(8,128)}, f32[256,256]{1,0:T(8,128)S(1)}, u32[]{:S(2)}) copy-start(f32[256,256]{1,0:T(8,128)S(1)} %get-tuple-element.6) | copy-start | bytes 786436
  23.0 1.8 copy-start.7
  55.7 11.7 %copy-start = (s32[1,48,64,256]{3,2,1,0:T(8,128)S(1)}, s32[1,48,64,256]{3,2,1,0:T(8,128)}, u32[]{:S(2)}) copy-start(s32[1,48,64,256]{3,2,1,0:T(8,128)} %param.6) | copy-start | bytes 9437188
  61.6 7.9 %copy-start.5 = (f32[48,64,256]{2,1,0:T(8,128)}, f32[48,64,256]{2,1,0:T(8,128)S(1)}, u32[]{:S(2)}) copy-start(f32[48,64,256]{2,1,0:T(8,128)S(1)} %bitcast_divide_fusion.1) | copy-start | bytes 9437188
  61.7 11.9 %collective-permute-start.2 = (f32[10,64,256]{2,1,0:T(8,128)S(1)}, f32[10,64,256]{2,1,0:T(8,128)S(1)}, u32[]{:S(2)}, u32[]{:S(2)}) collective-permute-start(f32[10,64,256]{2,1,0:T(8,128)S(1)} %get-tuple-element.15), channel_id=1, source_target_pairs={{0,1},{1,2},{2,3},{3,4},{4,5},{5,6},{6,7},{8,9},{9,10},{10,11},{11... | collective-permute-start | bytes 1966088 | tf_op jit(solution)/shard_map/ppermute | solution.py:17
  64.9 10.5 %collective-permute-start.3 = (f32[10,64,256]{2,1,0:T(8,128)S(1)}, f32[10,64,256]{2,1,0:T(8,128)S(1)}, u32[]{:S(2)}, u32[]{:S(2)}) collective-permute-start(f32[10,64,256]{2,1,0:T(8,128)S(1)} %get-tuple-element.16), channel_id=1, source_target_pairs={{1,0},{2,1},{3,2},{4,3},{5,4},{6,5},{7,6},{9,8},{10,9},{11,10},{12... | collective-permute-start | bytes 1966088 | tf_op jit(solution)/shard_map/ppermute | solution.py:19
  73.6 1.8 copy-start.9
  75.4 0.8 copy-start.11
  127.0 366.3 %all-reduce.4.cloned.1.call-start = ((), (), s32[]{:S(2)}) async-start(), calls=%async_computation | async-start | bytes 6291456 | tf_op jit(solution)/shard_map/psum | solution.py:64
  271.9 1.7 copy-start.2
  273.7 11.9 %collective-permute-start.4 = (f32[10,64,256]{2,1,0:T(8,128)S(1)}, f32[10,64,256]{2,1,0:T(8,128)S(1)}, u32[]{:S(2)}, u32[]{:S(2)}) collective-permute-start(f32[10,64,256]{2,1,0:T(8,128)S(1)} %get-tuple-element.13), channel_id=1, source_target_pairs={{0,1},{1,2},{2,3},{3,4},{4,5},{5,6},{6,7},{8,9},{9,10},{10,11},{11... | collective-permute-start | bytes 1966088 | tf_op jit(solution)/shard_map/ppermute | solution.py:17
  275.6 11.7 %collective-permute-start.5 = (f32[10,64,256]{2,1,0:T(8,128)S(1)}, f32[10,64,256]{2,1,0:T(8,128)}, u32[]{:S(2)}, u32[]{:S(2)}) collective-permute-start(f32[10,64,256]{2,1,0:T(8,128)S(1)} %get-tuple-element.14), channel_id=1, source_target_pairs={{1,0},{2,1},{3,2},{4,3},{5,4},{6,5},{7,6},{9,8},{10,9},{11,10},{12... | collective-permute-start | bytes 1966088 | tf_op jit(solution)/shard_map/ppermute | solution.py:19
  285.6 0.8 copy-start.10
  338.3 12.3 %copy-start.4 = (f32[48,64,256]{2,1,0:T(8,128)}, f32[48,64,256]{2,1,0:T(8,128)S(1)}, u32[]{:S(2)}) copy-start(f32[48,64,256]{2,1,0:T(8,128)S(1)} %bitcast_divide_fusion) | copy-start | bytes 9437188
  338.4 12.2 %collective-permute-start.6 = (f32[10,64,256]{2,1,0:T(8,128)S(1)}, f32[10,64,256]{2,1,0:T(8,128)S(1)}, u32[]{:S(2)}, u32[]{:S(2)}) collective-permute-start(f32[10,64,256]{2,1,0:T(8,128)S(1)} %get-tuple-element.11), channel_id=1, source_target_pairs={{0,1},{1,2},{2,3},{3,4},{4,5},{5,6},{6,7},{8,9},{9,10},{10,11},{11... | collective-permute-start | bytes 1966088 | tf_op jit(solution)/shard_map/ppermute | solution.py:17
  342.2 10.2 %collective-permute-start.7 = (f32[10,64,256]{2,1,0:T(8,128)S(1)}, f32[10,64,256]{2,1,0:T(8,128)}, u32[]{:S(2)}, u32[]{:S(2)}) collective-permute-start(f32[10,64,256]{2,1,0:T(8,128)S(1)} %get-tuple-element.12), channel_id=1, source_target_pairs={{1,0},{2,1},{3,2},{4,3},{5,4},{6,5},{7,6},{9,8},{10,9},{11,10},{12... | collective-permute-start | bytes 1966088 | tf_op jit(solution)/shard_map/ppermute | solution.py:19
  350.6 0.9 copy-start.8
  405.3 88.0 %copy-start.3 = (f32[48,64,256]{2,1,0:T(8,128)S(1)}, f32[48,64,256]{2,1,0:T(8,128)}, u32[]{:S(2)}) copy-start(f32[48,64,256]{2,1,0:T(8,128)} %copy-done.2) | copy-start | bytes 9437188
Sparse Core Ops, SparseCore 0:
  127.1 140.0 all-reduce.5
  405.4 87.8 all-reduce.3
where the time goes:
time: 509 us; the launch traced here: 506 us
  waiting for transfers between devices  250 us (49%)
  matrix products  191 us (38%)
  starting transfers between devices  23.2 us (5%)
  other arithmetic  15.2 us (3%)
  between operations  13.7 us (3%)
  local copies, waits for them, and re-layouts  12 us (2%)
    dot_general x4, matrix products, sweep_rest(): jnp.einsum('ij,xjz->xiz', along_y, volume, precision=lax.Precision.HIGHEST)  167 us
    psum x1, waiting for transfers between devices, body(): lax.psum(jnp.sum(weight_mask.astype(jnp.float32), axis=0), 'view')  140 us
    psum x1, waiting for transfers between devices, body(): summed = lax.psum(numerator, 'view')  88 us
    dot_general x4, matrix products, sweep_rest(): jnp.einsum('xyj,kj->xyk', volume, along_z, precision=lax.Precision.HIGHEST)  24.1 us
    ppermute x4, waiting for transfers between devices, extended(): lax.ppermute(tail, axis, [(i, (i + 1) % count) for i in range(ends)])  18.6 us
    ppermute x4, starting transfers between devices, extended(): lax.ppermute(head, axis, [((i + 1) % count, i) for i in range(ends)])  12.4 us
    ppermute x4, starting transfers between devices, extended(): lax.ppermute(tail, axis, [(i, (i + 1) % count) for i in range(ends)])  10.8 us
    div x2, other arithmetic, body(): estimate = estimate * summed / weights_all  10.4 us
  transfers between devices with their start and end apart: 10, of which 10 were waited for; matrix products, arithmetic and copies ran while one was open for 2% of the time, Pallas kernels for 0%

commit v1 on v0

v1 whole, which is shorter than its diff:
```python
import functools

import jax
import jax.numpy as jnp
from jax import lax
from jax.experimental import pallas as pl
from jax.experimental.pallas import tpu as pltpu
from jax.sharding import PartitionSpec as P

ITERS = 2
MESH = pl.DeviceIdType.MESH
F32, BF16 = jnp.float32, jnp.bfloat16


def split(value):
    high = value.astype(BF16)
    return high, (value - high.astype(F32)).astype(BF16)


def band(taps, row, size, row_sign):
    rows = lax.broadcasted_iota(jnp.int32, (size, size), 0)
    cols = lax.broadcasted_iota(jnp.int32, (size, size), 1)
    count = taps.shape[1]
    offset = (cols - rows) * row_sign + (count - 1) // 2
    total = jnp.zeros((size, size), F32)
    for k in range(count):
        total = jnp.where(offset == k, taps[row, k], total)
    return split(total)


def kernel(dims, taps, est_in, seen_in, mask_in, out,
           ext, seen, mask, wf, wsum, nums, recvs, ybuf, ymats, zmats,
           load_sem, halo_send, halo_recv, rs_send, rs_recv, ag_send, ag_recv):
    views, blks, bits = dims
    slab, cy, cz = seen.shape
    count = taps.shape[1]
    rad = (count - 1) // 2
    part = slab // bits
    chunk = part // 2
    chunks = 2 * bits
    v, b = lax.axis_index("view"), lax.axis_index("blk")
    bit = [(v // 2**p) % 2 for p in range(bits)]
    partner = [v + (1 - 2 * bit[p]) * 2**p for p in range(bits)]
    left, right = (b + blks - 1) % blks, (b + 1) % blks

    loads = [
        pltpu.make_async_copy(est_in, ext.at[0, pl.ds(rad, slab)], load_sem.at[0]),
        pltpu.make_async_copy(mask_in.at[0], mask, load_sem.at[1]),
        pltpu.make_async_copy(seen_in.at[0], seen, load_sem.at[2]),
    ]
    for load in loads:
        load.start()

    barrier = pltpu.get_barrier_semaphore()
    for p in range(bits):
        pl.semaphore_signal(barrier, inc=1, device_id=(partner[p], b), device_id_type=MESH)
    for near in (left, right):
        pl.semaphore_signal(barrier, inc=1, device_id=(v, near), device_id_type=MESH)
    pl.semaphore_wait(barrier, bits + 2)

    def halo(which, side):
        start, land, near = ((slab, 0, right), (rad, rad + slab, left))[side]
        return pltpu.make_async_remote_copy(
            src_ref=ext.at[which, pl.ds(start, rad)], dst_ref=ext.at[which, pl.ds(land, rad)],
            send_sem=halo_send.at[which, side], recv_sem=halo_recv.at[which, side],
            device_id=(v, near), device_id_type=MESH)

    def halo_start(which):
        @pl.when(b < blks - 1)
        def _():
            halo(which, 0).start()

        @pl.when(b > 0)
        def _():
            halo(which, 1).start()

    def halo_wait(which):
        @pl.when(b > 0)
        def _():
            halo(which, 0).wait_recv()

        @pl.when(b == 0)
        def _():
            ext[which, pl.ds(0, rad)] = jnp.zeros((rad, cy, cz), F32)

        @pl.when(b < blks - 1)
        def _():
            halo(which, 1).wait_recv()

        @pl.when(b == blks - 1)
        def _():
            ext[which, pl.ds(rad + slab, rad)] = jnp.zeros((rad, cy, cz), F32)

    def halo_sent(which):
        @pl.when(b < blks - 1)
        def _():
            halo(which, 0).wait_send()

        @pl.when(b > 0)
        def _():
            halo(which, 1).wait_send()

    def region(p, s):
        start, length = p * part, part
        for t in range(s):
            length //= 2
            start = start + bit[(p + t) % bits] * length
        return start, length

    def rs_slot(s, p):
        length = part // 2 ** (s + 1)
        return bits * (part - part // 2**s) + p * length, length

    def rs_copy(r, s, p):
        buf = wsum if r == 0 else nums.at[r - 1]
        start, length = region(p, s)
        length //= 2
        mine = bit[(p + s) % bits]
        slot, _ = rs_slot(s, p)
        return pltpu.make_async_remote_copy(
            src_ref=buf.at[pl.ds(start + (1 - mine) * length, length)],
            dst_ref=recvs.at[r, pl.ds(slot, length)],
            send_sem=rs_send.at[r, s, p], recv_sem=rs_recv.at[r, s, p],
            device_id=(partner[(p + s) % bits], b), device_id_type=MESH)

    def rs_take(r, s, p):
        buf = wsum if r == 0 else nums.at[r - 1]
        rs_copy(r, s, p).wait_recv()
        start, length = region(p, s + 1)
        slot, _ = rs_slot(s, p)

        def add(i, carry):
            buf[start + i] = buf[start + i] + recvs[r, slot + i]
            return carry

        lax.fori_loop(0, length, add, 0)

    def ag_copy(r, s, p):
        start, length = region(p, s + 1)
        if r < ITERS - 1:
            ref = ext.at[2 * (r + 1), pl.ds(start + rad, length)]
        else:
            ref = out.at[pl.ds(start, length)]
        return pltpu.make_async_remote_copy(
            src_ref=ref, dst_ref=ref,
            send_sem=ag_send.at[r, s, p], recv_sem=ag_recv.at[r, s, p],
            device_id=(partner[(p + s) % bits], b), device_id_type=MESH)

    def blur(which, c, back):
        first = c * chunk

        def pair(j, carry):
            base = first + 2 * j
            one = two = None
            for k in range(count + 1):
                plane = ext[which, base + k]
                if k < count:
                    term = taps[0, count - 1 - k if back else k] * plane
                    one = term if one is None else one + term
                if k > 0:
                    term = taps[0, count - k if back else k - 1] * plane
                    two = term if two is None else two + term
            for half, plane in enumerate((one, two)):
                high, low = split(plane)
                stack = jnp.concatenate([high, high, low], axis=0)
                ybuf[pl.ds((2 * j + half) * cy, cy)] = jnp.dot(
                    ymats[back], stack, preferred_element_type=F32)
            return carry

        lax.fori_loop(0, chunk // 2, pair, 0)
        high, low = split(ybuf[...])
        high_mat, low_mat = zmats[back, 0], zmats[back, 1]
        result = jnp.dot(high, high_mat, preferred_element_type=F32)
        result += jnp.dot(low, high_mat, preferred_element_type=F32)
        result += jnp.dot(high, low_mat, preferred_element_type=F32)
        return result.reshape(chunk, cy, cz)

    inner = [c for c in range(chunks) if c * chunk >= rad and (c + 1) * chunk <= slab - rad]
    low_c, high_c = (inner[0], inner[-1] + 1) if inner else (0, 0)

    def over_inner(step):
        if inner:
            def run(c, carry):
                step(c)
                return carry

            lax.fori_loop(low_c, high_c, run, 0)

    def over_edges(step):
        def run(t, carry):
            step(t + (t // max(low_c, 1)) * (high_c - low_c) if 2 * low_c == chunks - (high_c - low_c) else t)
            return carry

        lax.fori_loop(0, chunks - (high_c - low_c), run, 0)

    loads[0].wait()
    halo_start(0)
    loads[1].wait()

    def to_float(i, carry):
        weights = mask[i].astype(F32)
        wf[i] = weights
        wsum[i] = weights
        return carry

    lax.fori_loop(0, slab, to_float, 0)
    for p in range(bits):
        rs_copy(0, 0, p).start()

    for back in range(2):
        sign = -1 if back else 1
        high, low = band(taps, 1, cy, sign)
        ymats[back] = jnp.concatenate([high, low, high], axis=1)
        high, low = band(taps, 2, cz, -sign)
        zmats[back, 0] = high
        zmats[back, 1] = low
    loads[2].wait()

    for r in range(ITERS):
        here, there = 2 * r, 2 * r + 1

        def quotient(c):
            blurred = blur(here, c, 0)
            rows = pl.ds(c * chunk, chunk)
            ext[there, pl.ds(rad + c * chunk, chunk)] = seen[rows] / blurred

        over_inner(quotient)
        halo_wait(here)
        over_edges(quotient)
        halo_start(there)
        if r == 0:
            for p in range(bits):
                rs_take(0, 0, p)
                if bits > 1:
                    rs_copy(0, 1, p).start()

        def correct(c):
            corrected = blur(there, c, 1)
            rows = pl.ds(c * chunk, chunk)
            nums[r, rows] = wf[rows] * corrected
            for p in range(bits):
                @pl.when(c == 2 * p + 1 - bit[p])
                def _(p=p):
                    rs_copy(r + 1, 0, p).start()

        over_inner(correct)
        halo_wait(there)
        over_edges(correct)
        if r == 0:
            for s in range(1, bits):
                for p in range(bits):
                    rs_take(0, s, p)
                    if s + 1 < bits:
                        rs_copy(0, s + 1, p).start()
        for s in range(bits):
            for p in range(bits):
                rs_take(r + 1, s, p)
                if s + 1 < bits:
                    rs_copy(r + 1, s + 1, p).start()
                else:
                    start, length = region(p, bits)

                    def update(i, carry):
                        cell = start + i
                        fresh = ext[here, rad + cell] * nums[r, cell] / wsum[cell]
                        if r < ITERS - 1:
                            ext[here + 2, rad + cell] = fresh
                        else:
                            out[cell] = fresh
                        return carry

                    lax.fori_loop(0, length, update, 0)
                    ag_copy(r, s, p).start()
        for s in range(bits - 1, -1, -1):
            for p in range(bits):
                ag_copy(r, s, p).wait_recv()
                if s > 0:
                    ag_copy(r, s - 1, p).start()
        if r < ITERS - 1:
            halo_start(here + 2)

    for which in range(2 * ITERS):
        halo_sent(which)
    for s in range(bits):
        for p in range(bits):
            for r in range(ITERS + 1):
                rs_copy(r, s, p).wait_send()
            for r in range(ITERS):
                ag_copy(r, s, p).wait_send()


def body(views, blks, estimate, views_seen, weight_mask, psf):
    slab, cy, cz = estimate.shape
    bits = views.bit_length() - 1
    count = psf.shape[-1]
    rad = (count - 1) // 2
    chunk = slab // bits // 2
    taps = (psf / jnp.sum(psf, axis=-1, keepdims=True))[0]
    hbm = pl.BlockSpec(memory_space=pl.ANY)
    vmem = pltpu.VMEM
    dma = pltpu.SemaphoreType.DMA
    landing = bits * (slab // bits - slab // bits // views)
    return pl.pallas_call(
        functools.partial(kernel, (views, blks, bits)),
        out_shape=jax.ShapeDtypeStruct(estimate.shape, F32),
        in_specs=[pl.BlockSpec(memory_space=pltpu.SMEM), hbm, hbm, hbm],
        out_specs=pl.BlockSpec(memory_space=pltpu.VMEM),
        scratch_shapes=[
            vmem((2 * ITERS, slab + 2 * rad, cy, cz), F32),
            vmem((slab, cy, cz), F32),
            vmem((slab, cy, cz), jnp.int32),
            vmem((slab, cy, cz), F32),
            vmem((slab, cy, cz), F32),
            vmem((ITERS, slab, cy, cz), F32),
            vmem((ITERS + 1, landing, cy, cz), F32),
            vmem((chunk * cy, cz), F32),
            vmem((2, cy, 3 * cy), BF16),
            vmem((2, 2, cz, cz), BF16),
            dma((3,)),
            dma((2 * ITERS, 2)),
            dma((2 * ITERS, 2)),
            dma((ITERS + 1, bits, bits)),
            dma((ITERS + 1, bits, bits)),
            dma((ITERS, bits, bits)),
            dma((ITERS, bits, bits)),
        ],
        compiler_params=pltpu.CompilerParams(
            collective_id=0, has_side_effects=True, vmem_limit_bytes=60 * 2**20),
    )(taps, estimate, views_seen, weight_mask)


def solution(mesh):
    placed = (
        P("blk", None, None),
        P("view", "blk", None, None),
        P("view", "blk", None, None),
        P("view", None, None),
    )
    return jax.shard_map(
        functools.partial(body, mesh.shape["view"], mesh.shape["blk"]),
        mesh=mesh, in_specs=placed, out_specs=P("blk", None, None), check_vma=False
    )
```

time: 509 us -> 175 us (0.34)
  waiting for transfers between devices: 250 us -> 0 us
  matrix products: 191 us -> 0 us
  Pallas kernels: 0 us -> 169 us
  starting transfers between devices: 23.2 us -> 0 us
  between operations: 13.7 us -> 0.01 us
  other arithmetic: 15.2 us -> 1.54 us
  local copies, waits for them, and re-layouts: 12 us -> 4.49 us
    psum x2 -> x0, waiting for transfers between devices: 228 us -> none  [the longest x1 140 us: body(): lax.psum(jnp.sum(weight_mask.astype(jnp.float32), axis=0), 'view')]
    dot_general x8 -> x0, matrix products: 191 us -> none  [the longest x4 167 us: sweep_rest(): jnp.einsum('ij,xjz->xiz', along_y, volume, precision=lax.Precision.HIGHEST)]
    pallas_call x0 -> x1, Pallas kernels: none -> 169 us  [body(): pl.pallas_call(functools.partial(kernel, (views, blks, bits)), out_shape=...]
    ppermute x8 -> x0, starting transfers between devices: 23.2 us -> none  [the longest x4 12.4 us: extended(): lax.ppermute(head, axis, [((i + 1) % count, i) for i in range(ends)])]
    ppermute x8 -> x0, waiting for transfers between devices: 22.2 us -> none  [the longest x4 18.6 us: extended(): lax.ppermute(tail, axis, [(i, (i + 1) % count) for i in range(ends)])]
    div x3 -> x1, other arithmetic: 11.1 us -> 0.75 us  [body(): taps = (psf / jnp.sum(psf, axis=-1, keepdims=True))[0]]
  transfers between devices with their start and end apart: 10 -> 0, of which waited for: 10 -> 0; matrix products, arithmetic and copies ran while one was open for 2% -> 0% of each run, Pallas kernels for 0% -> 0%
where the time goes in v1:
time: 175 us
  Pallas kernels  169 us (97%)
  local copies, waits for them, and re-layouts  4.49 us (3%)
    pallas_call x1, Pallas kernels, body(): pl.pallas_call(functools.partial(kernel, (views, blks, bits)), out_shape=...  169 us
    unnamed x2, local copies, waits for them, and re-layouts  4.49 us

profile of v1, /device:TPU:20, one launch (start us, length us, event | category | flops | bytes accessed | tf_op | source)
XLA Modules:
  0.0 174.9 jit_solution(7620438608080605984)
XLA Ops:
  0.0 0.8 reduce_sum.9
  0.8 0.8 broadcast_divide_fusion
  1.5 0.6 copy.7
  2.1 168.8 %shard_map.46 = f32[48,64,256]{2,1,0:T(8,128)} custom-call(f32[3,21]{1,0:T(4,128)} %bitcast.3, f32[48,64,256]{2,1,0:T(8,128)} %est_in.1, f32[1,48,64,256]{3,2,1,0:T(8,128)} %seen_in.1, s32[1,48,64,256]{3,2,1,0:T(8,128)} %mask_in.1), custom_call_target="tpu_custom_call" | custom-call | tf_op jit(solution)/shard_map/pallas_call | solution.py:303
  171.0 3.9 %copy.9 = f32[48,64,256]{2,1,0:T(8,128)} copy(f32[48,64,256]{2,1,0:T(8,128)} %shard_map.46) | data formatting | bytes 6291456

commit v2 on v1

--- a/solution.py
+++ b/solution.py
@@ -17,27 +17,30 @@
     return high, (value - high.astype(F32)).astype(BF16)
 
 
-def band(taps, row, size, row_sign):
+def band(taps, row, size, row_sign, scale):
     rows = lax.broadcasted_iota(jnp.int32, (size, size), 0)
     cols = lax.broadcasted_iota(jnp.int32, (size, size), 1)
-    count = taps.shape[1]
+    count = taps.shape[2]
     offset = (cols - rows) * row_sign + (count - 1) // 2
     total = jnp.zeros((size, size), F32)
     for k in range(count):
-        total = jnp.where(offset == k, taps[row, k], total)
-    return split(total)
-
-
-def kernel(dims, taps, est_in, seen_in, mask_in, out,
+        total = jnp.where(offset == k, taps[0, row, k], total)
+    return split(total * scale)
+
+
+def kernel(dims, taps, est_in, seen_in, mask_in, out, final,
            ext, seen, mask, wf, wsum, nums, recvs, ybuf, ymats, zmats,
-           load_sem, halo_send, halo_recv, rs_send, rs_recv, ag_send, ag_recv):
+           load_sem, store_sem, halo_send, halo_recv, rs_send, rs_recv, ag_send, ag_recv):
     views, blks, bits = dims
     slab, cy, cz = seen.shape
-    count = taps.shape[1]
+    count = taps.shape[2]
     rad = (count - 1) // 2
-    part = slab // bits
-    chunk = part // 2
     chunks = 2 * bits
+    chunk = slab // chunks
+    inner = [c for c in range(chunks) if c * chunk >= rad and (c + 1) * chunk <= slab - rad]
+    edges = [c for c in range(chunks) if c not in inner]
+    order = edges + inner
+    turn = [order.index(c) % bits for c in range(chunks)]
     v, b = lax.axis_index("view"), lax.axis_index("blk")
     bit = [(v // 2**p) % 2 for p in range(bits)]
     partner = [v + (1 - 2 * bit[p]) * 2**p for p in range(bits)]
@@ -100,28 +103,31 @@
         def _():
             halo(which, 1).wait_send()
 
+    def way(p, s):
+        return (turn[p] + s) % bits
+
     def region(p, s):
-        start, length = p * part, part
+        start, length = p * chunk, chunk
         for t in range(s):
             length //= 2
-            start = start + bit[(p + t) % bits] * length
+            start = start + bit[way(p, t)] * length
         return start, length
 
     def rs_slot(s, p):
-        length = part // 2 ** (s + 1)
-        return bits * (part - part // 2**s) + p * length, length
+        length = chunk // 2 ** (s + 1)
+        return chunks * (chunk - chunk // 2**s) + p * length, length
 
     def rs_copy(r, s, p):
         buf = wsum if r == 0 else nums.at[r - 1]
         start, length = region(p, s)
         length //= 2
-        mine = bit[(p + s) % bits]
+        mine = bit[way(p, s)]
         slot, _ = rs_slot(s, p)
         return pltpu.make_async_remote_copy(
             src_ref=buf.at[pl.ds(start + (1 - mine) * length, length)],
             dst_ref=recvs.at[r, pl.ds(slot, length)],
             send_sem=rs_send.at[r, s, p], recv_sem=rs_recv.at[r, s, p],
-            device_id=(partner[(p + s) % bits], b), device_id_type=MESH)
+            device_id=(partner[way(p, s)], b), device_id_type=MESH)
 
     def rs_take(r, s, p):
         buf = wsum if r == 0 else nums.at[r - 1]
@@ -140,11 +146,15 @@
         if r < ITERS - 1:
             ref = ext.at[2 * (r + 1), pl.ds(start + rad, length)]
         else:
-            ref = out.at[pl.ds(start, length)]
+            ref = final.at[pl.ds(start, length)]
         return pltpu.make_async_remote_copy(
             src_ref=ref, dst_ref=ref,
             send_sem=ag_send.at[r, s, p], recv_sem=ag_recv.at[r, s, p],
-            device_id=(partner[(p + s) % bits], b), device_id_type=MESH)
+            device_id=(partner[way(p, s)], b), device_id_type=MESH)
+
+    def store(p):
+        rows = pl.ds(p * chunk, chunk)
+        return pltpu.make_async_copy(final.at[rows], out.at[rows], store_sem.at[p])
 
     def blur(which, c, back):
         first = c * chunk
@@ -155,10 +165,10 @@
             for k in range(count + 1):
                 plane = ext[which, base + k]
                 if k < count:
-                    term = taps[0, count - 1 - k if back else k] * plane
+                    term = taps[0, 0, count - 1 - k if back else k] * plane
                     one = term if one is None else one + term
                 if k > 0:
-                    term = taps[0, count - k if back else k - 1] * plane
+                    term = taps[0, 0, count - k if back else k - 1] * plane
                     two = term if two is None else two + term
             for half, plane in enumerate((one, two)):
                 high, low = split(plane)
@@ -175,23 +185,23 @@
         result += jnp.dot(high, low_mat, preferred_element_type=F32)
         return result.reshape(chunk, cy, cz)
 
-    inner = [c for c in range(chunks) if c * chunk >= rad and (c + 1) * chunk <= slab - rad]
-    low_c, high_c = (inner[0], inner[-1] + 1) if inner else (0, 0)
+    low_c = inner[0] if inner else 0
+    gap = len(inner)
 
     def over_inner(step):
+        def run(c, carry):
+            step(c)
+            return carry
+
         if inner:
-            def run(c, carry):
-                step(c)
-                return carry
-
-            lax.fori_loop(low_c, high_c, run, 0)
+            lax.fori_loop(low_c, low_c + gap, run, 0)
 
     def over_edges(step):
         def run(t, carry):
-            step(t + (t // max(low_c, 1)) * (high_c - low_c) if 2 * low_c == chunks - (high_c - low_c) else t)
+            step(t + (t // low_c) * gap if inner else t)
             return carry
 
-        lax.fori_loop(0, chunks - (high_c - low_c), run, 0)
+        lax.fori_loop(0, len(edges), run, 0)
 
     loads[0].wait()
     halo_start(0)
@@ -204,14 +214,22 @@
         return carry
 
     lax.fori_loop(0, slab, to_float, 0)
-    for p in range(bits):
+    for p in order:
         rs_copy(0, 0, p).start()
 
+    sums = []
+    for row in range(3):
+        total = taps[0, row, 0]
+        for k in range(1, count):
+            total = total + taps[0, row, k]
+        sums.append(jnp.full((1, cz), total, F32))
+    y_scale = (1.0 / (sums[0] * sums[1]))[:, :cy]
+    z_scale = 1.0 / sums[2]
     for back in range(2):
         sign = -1 if back else 1
-        high, low = band(taps, 1, cy, sign)
+        high, low = band(taps, 1, cy, sign, y_scale)
         ymats[back] = jnp.concatenate([high, low, high], axis=1)
-        high, low = band(taps, 2, cz, -sign)
+        high, low = band(taps, 2, cz, -sign, z_scale)
         zmats[back, 0] = high
         zmats[back, 1] = low
     loads[2].wait()
@@ -224,12 +242,12 @@
             rows = pl.ds(c * chunk, chunk)
             ext[there, pl.ds(rad + c * chunk, chunk)] = seen[rows] / blurred
 
-        over_inner(quotient)
         halo_wait(here)
         over_edges(quotient)
         halo_start(there)
+        over_inner(quotient)
         if r == 0:
-            for p in range(bits):
+            for p in order:
                 rs_take(0, 0, p)
                 if bits > 1:
                     rs_copy(0, 1, p).start()
@@ -238,51 +256,65 @@
             corrected = blur(there, c, 1)
             rows = pl.ds(c * chunk, chunk)
             nums[r, rows] = wf[rows] * corrected
-            for p in range(bits):
-                @pl.when(c == 2 * p + 1 - bit[p])
+            for p in range(chunks):
+                @pl.when(c == p)
                 def _(p=p):
                     rs_copy(r + 1, 0, p).start()
 
-        over_inner(correct)
         halo_wait(there)
         over_edges(correct)
+        over_inner(correct)
         if r == 0:
             for s in range(1, bits):
-                for p in range(bits):
+                for p in order:
                     rs_take(0, s, p)
                     if s + 1 < bits:
                         rs_copy(0, s + 1, p).start()
-        for s in range(bits):
-            for p in range(bits):
-                rs_take(r + 1, s, p)
-                if s + 1 < bits:
-                    rs_copy(r + 1, s + 1, p).start()
+
+        def update(p):
+            start, length = region(p, bits)
+
+            def cells(i, carry):
+                cell = start + i
+                fresh = ext[here, rad + cell] * nums[r, cell] / wsum[cell]
+                if r < ITERS - 1:
+                    ext[here + 2, rad + cell] = fresh
                 else:
-                    start, length = region(p, bits)
-
-                    def update(i, carry):
-                        cell = start + i
-                        fresh = ext[here, rad + cell] * nums[r, cell] / wsum[cell]
-                        if r < ITERS - 1:
-                            ext[here + 2, rad + cell] = fresh
-                        else:
-                            out[cell] = fresh
-                        return carry
-
-                    lax.fori_loop(0, length, update, 0)
-                    ag_copy(r, s, p).start()
-        for s in range(bits - 1, -1, -1):
-            for p in range(bits):
+                    final[cell] = fresh
+                return carry
+
+            lax.fori_loop(0, length, cells, 0)
+
+        events = [(e, pos) for e in range(2 * bits) for pos in range(chunks)]
+        events.sort(key=lambda ev: (ev[0] + ev[1] // bits, -(ev[1] // bits), ev[1] % bits))
+        arrived = set()
+        for e, pos in events:
+            p = order[pos]
+            if e < bits:
+                rs_take(r + 1, e, p)
+                if e + 1 < bits:
+                    rs_copy(r + 1, e + 1, p).start()
+                else:
+                    update(p)
+                    ag_copy(r, bits - 1, p).start()
+            else:
+                s = 2 * bits - 1 - e
                 ag_copy(r, s, p).wait_recv()
                 if s > 0:
                     ag_copy(r, s - 1, p).start()
-        if r < ITERS - 1:
-            halo_start(here + 2)
-
+                elif r < ITERS - 1:
+                    if not set(edges) <= arrived and set(edges) <= arrived | {p}:
+                        halo_start(here + 2)
+                    arrived.add(p)
+                else:
+                    store(p).start()
+
+    for p in range(chunks):
+        store(p).wait()
     for which in range(2 * ITERS):
         halo_sent(which)
     for s in range(bits):
-        for p in range(bits):
+        for p in range(chunks):
             for r in range(ITERS + 1):
                 rs_copy(r, s, p).wait_send()
             for r in range(ITERS):
@@ -294,18 +326,19 @@
     bits = views.bit_length() - 1
     count = psf.shape[-1]
     rad = (count - 1) // 2
-    chunk = slab // bits // 2
-    taps = (psf / jnp.sum(psf, axis=-1, keepdims=True))[0]
+    chunk = slab // (2 * bits)
     hbm = pl.BlockSpec(memory_space=pl.ANY)
     vmem = pltpu.VMEM
     dma = pltpu.SemaphoreType.DMA
-    landing = bits * (slab // bits - slab // bits // views)
+    landing = slab - slab // views
+    chunks = 2 * bits
     return pl.pallas_call(
         functools.partial(kernel, (views, blks, bits)),
         out_shape=jax.ShapeDtypeStruct(estimate.shape, F32),
         in_specs=[pl.BlockSpec(memory_space=pltpu.SMEM), hbm, hbm, hbm],
-        out_specs=pl.BlockSpec(memory_space=pltpu.VMEM),
+        out_specs=hbm,
         scratch_shapes=[
+            vmem((slab, cy, cz), F32),
             vmem((2 * ITERS, slab + 2 * rad, cy, cz), F32),
             vmem((slab, cy, cz), F32),
             vmem((slab, cy, cz), jnp.int32),
@@ -317,16 +350,17 @@
             vmem((2, cy, 3 * cy), BF16),
             vmem((2, 2, cz, cz), BF16),
             dma((3,)),
+            dma((chunks,)),
             dma((2 * ITERS, 2)),
             dma((2 * ITERS, 2)),
-            dma((ITERS + 1, bits, bits)),
-            dma((ITERS + 1, bits, bits)),
-            dma((ITERS, bits, bits)),
-            dma((ITERS, bits, bits)),
+            dma((ITERS + 1, bits, chunks)),
+            dma((ITERS + 1, bits, chunks)),
+            dma((ITERS, bits, chunks)),
+            dma((ITERS, bits, chunks)),
         ],
         compiler_params=pltpu.CompilerParams(
             collective_id=0, has_side_effects=True, vmem_limit_bytes=60 * 2**20),
-    )(taps, estimate, views_seen, weight_mask)
+    )(psf, estimate, views_seen, weight_mask)
 
 
 def solution(mesh):

time: 175 us -> 164 us (0.937)
  Pallas kernels: 169 us -> 157 us
    pallas_call x1, Pallas kernels: 169 us -> 157 us  [body(): pl.pallas_call(functools.partial(kernel, (views, blks, bits)), out_shape=...]
where the time goes in v2:
time: 164 us; the launch traced here: 163 us
  Pallas kernels  157 us (96%)
  local copies, waits for them, and re-layouts  5.17 us (3%)
    pallas_call x1, Pallas kernels, body(): pl.pallas_call(functools.partial(kernel, (views, blks, bits)), out_shape=...  157 us
    unnamed x2, local copies, waits for them, and re-layouts  5.17 us

profile of v2, /device:TPU:20, one launch (start us, length us, event | category | flops | bytes accessed | tf_op | source)
XLA Modules:
  0.0 162.6 jit_solution(11824369927872562526)
XLA Ops:
  0.0 1.3 copy.5.taps
  1.3 157.5 %shard_map.46 = f32[48,64,256]{2,1,0:T(8,128)} custom-call(f32[1,3,21]{2,1,0:T(4,128)} %copy.5.taps, f32[48,64,256]{2,1,0:T(8,128)} %est_in.1, f32[1,48,64,256]{3,2,1,0:T(8,128)} %seen_in.1, s32[1,48,64,256]{3,2,1,0:T(8,128)} %mask_in.1), custom_call_target="tpu_custom_call" | custom-call | tf_op jit(solution)/shard_map/pallas_call | solution.py:335
  158.7 3.9 %copy.7 = f32[48,64,256]{2,1,0:T(8,128)} copy(f32[48,64,256]{2,1,0:T(8,128)} %shard_map.46) | data formatting | bytes 6291456

commit v3 on v2

--- a/solution.py
+++ b/solution.py
@@ -29,7 +29,7 @@
 
 
 def kernel(dims, taps, est_in, seen_in, mask_in, out, final,
-           ext, seen, mask, wf, wsum, nums, recvs, ybuf, ymats, zmats,
+           ext, seen, mask, wf, wsum, nums, recvs, xbuf, ymats, zmats,
            load_sem, store_sem, halo_send, halo_recv, rs_send, rs_recv, ag_send, ag_recv):
     views, blks, bits = dims
     slab, cy, cz = seen.shape
@@ -159,26 +159,30 @@
     def blur(which, c, back):
         first = c * chunk
 
-        def pair(j, carry):
-            base = first + 2 * j
-            one = two = None
-            for k in range(count + 1):
-                plane = ext[which, base + k]
-                if k < count:
-                    term = taps[0, 0, count - 1 - k if back else k] * plane
-                    one = term if one is None else one + term
-                if k > 0:
-                    term = taps[0, 0, count - k if back else k - 1] * plane
-                    two = term if two is None else two + term
-            for half, plane in enumerate((one, two)):
-                high, low = split(plane)
-                stack = jnp.concatenate([high, high, low], axis=0)
-                ybuf[pl.ds((2 * j + half) * cy, cy)] = jnp.dot(
-                    ymats[back], stack, preferred_element_type=F32)
+        height, lanes = 8, 256
+
+        def block(j, carry):
+            line = pl.multiple_of((j // (cz // lanes)) * height, height)
+            column = pl.multiple_of((j % (cz // lanes)) * lanes, lanes)
+            window = (pl.ds(line, height), pl.ds(column, lanes))
+            totals = [None] * chunk
+            for k in range(count + chunk - 1):
+                plane = ext[(which, first + k) + window]
+                for i in range(max(0, k - count + 1), min(chunk, k + 1)):
+                    tap = k - i
+                    term = taps[0, 0, count - 1 - tap if back else tap] * plane
+                    totals[i] = term if totals[i] is None else totals[i] + term
+            for i in range(chunk):
+                xbuf[(i,) + window] = totals[i]
             return carry
 
-        lax.fori_loop(0, chunk // 2, pair, 0)
-        high, low = split(ybuf[...])
+        lax.fori_loop(0, (cy // height) * (cz // lanes), block, 0)
+        blurred = []
+        for i in range(chunk):
+            high, low = split(xbuf[i])
+            stack = jnp.concatenate([high, high, low], axis=0)
+            blurred.append(jnp.dot(ymats[back], stack, preferred_element_type=F32))
+        high, low = split(jnp.concatenate(blurred, axis=0))
         high_mat, low_mat = zmats[back, 0], zmats[back, 1]
         result = jnp.dot(high, high_mat, preferred_element_type=F32)
         result += jnp.dot(low, high_mat, preferred_element_type=F32)
@@ -346,7 +350,7 @@
             vmem((slab, cy, cz), F32),
             vmem((ITERS, slab, cy, cz), F32),
             vmem((ITERS + 1, landing, cy, cz), F32),
-            vmem((chunk * cy, cz), F32),
+            vmem((chunk, cy, cz), F32),
             vmem((2, cy, 3 * cy), BF16),
             vmem((2, 2, cz, cz), BF16),
             dma((3,)),

time: 164 us -> 160 us (0.976)
  Pallas kernels: 157 us -> 154 us
    pallas_call x1, Pallas kernels: 157 us -> 154 us  [body(): pl.pallas_call(functools.partial(kernel, (views, blks, bits)), out_shape=...]
where the time goes in v3:
time: 160 us; the launch traced here: 159 us
  Pallas kernels  154 us (96%)
  local copies, waits for them, and re-layouts  5.17 us (3%)
    pallas_call x1, Pallas kernels, body(): pl.pallas_call(functools.partial(kernel, (views, blks, bits)), out_shape=...  154 us
    unnamed x2, local copies, waits for them, and re-layouts  5.17 us

profile of v3, /device:TPU:20, one launch (start us, length us, event | category | flops | bytes accessed | tf_op | source)
XLA Modules:
  0.0 159.0 jit_solution(11170868909759147419)
XLA Ops:
  0.0 1.3 copy.5.taps
  1.3 153.8 %shard_map.46 = f32[48,64,256]{2,1,0:T(8,128)} custom-call(f32[1,3,21]{2,1,0:T(4,128)} %copy.5.taps, f32[48,64,256]{2,1,0:T(8,128)} %est_in.1, f32[1,48,64,256]{3,2,1,0:T(8,128)} %seen_in.1, s32[1,48,64,256]{3,2,1,0:T(8,128)} %mask_in.1), custom_call_target="tpu_custom_call" | custom-call | tf_op jit(solution)/shard_map/pallas_call | solution.py:339
  155.1 3.9 %copy.7 = f32[48,64,256]{2,1,0:T(8,128)} copy(f32[48,64,256]{2,1,0:T(8,128)} %shard_map.46) | data formatting | bytes 6291456
